TPU v7x, 32 devices: a whole 2x2x4 slice. The times are simulated.
32 devices in a mesh: groups: 2 (over y), blk: 4 (over z), comp: 2 (over x), lat: 2 (over core).
Axes of the slice: x: 2, y: 2, z: 4, core: 2. Of those that a mesh axis runs over, the one named last changes fastest.
Arguments:
- rhs: float32 [96, 2, 4, 2048], P(('groups', 'comp'), None, 'blk'), parts along dimension 0, may hold values from -6 to 6
- legendre: bfloat16 [4, 2048, 32], P('blk', None, 'lat'), may hold values from -0.03125 to 0.03125
- beam: float32 [24, 2048], replicated, may hold values from 0.3 to 1
- mixing: float32 [24, 48], P(None, 'comp'), may hold values from -0.875 to 0.875
- prior: float32 [48, 2048], P('comp'), may hold values from 0.5 to 4
- inv_noise: float32 [24, 32, 4096], P('comp', ('blk', 'lat')), may hold values from 0.25 to 4
- mask_flags: int32 [24, 32], P('comp', ('blk', 'lat')), may hold values 0 or 1
- cycle_len: int32 [32], P('lat'), may hold values from 16 to 4096, as said below
- cycle_slot: int32 [32], P('lat'), may hold values from 0 to 15, as said below
- m_values: int32 [4], replicated, may hold values from 0 to 2047, as said below
Outputs:
- solution: float32 [96, 2, 4, 2048], P(('groups', 'comp'), None, 'blk'), parts along dimension 0
- residual: float32 [96, 2, 4, 2048], P(('groups', 'comp'), None, 'blk'), parts along dimension 0
There are 2 independent parts, one for each index of `groups`. A program takes and returns all parts, laid end to end along the dimension named above; an argument that names none is the same for every part. Nothing has to cross between parts.
Inputs may be any that keep to these rules, and one draw needn't show every extreme that they name: `cycle_len`: lengths are multiples of 4; each band (aligned block of 16 entries) holds a cycle of exactly 4096 pixels. `cycle_slot`: each aligned block of 16 entries is a permutation of 0 to 15. `m_values`: the m values are distinct, and both 0 and 2047 occur.
All inputs are finite; a program needn't handle non-finite values. No bound on the sum of `mask_flags` on one device may be relied on, other than what follows from the above.
Results may differ from a plain program's by a relative error of at most 0.023.
Values may be sent and summed in bfloat16 or wider, within the bound.
A program may use at most 64 MiB of HBM per device.

v0:
```python
import math

import jax
import jax.numpy as jnp
from jax import lax
from jax.sharding import PartitionSpec as P

ITERS = 3


HIGHEST_PRECISION = lax.Precision.HIGHEST


def cycle_table(m_values, length, pixel_count):
    pixels = jnp.arange(pixel_count, dtype=jnp.int32)
    phase_ids = m_values[:, None] * (2 * pixels[None, :] + 1) % (2 * length)
    angles = math.pi * phase_ids.astype(jnp.float32) / length.astype(jnp.float32)
    inside = (pixels < length)[None, :]
    cosine = jnp.where(inside, jnp.cos(angles), jnp.float32(0.0))
    sine_part = jnp.where(inside, -jnp.sin(angles), jnp.float32(0.0))
    return jnp.stack([cosine, sine_part]).astype(jnp.bfloat16)


def local(
    rhs, legendre, beam, mixing, prior, inv_noise, mask_flags, cycle_len, cycle_slot, m_values
):
    cycle_count = inv_noise.shape[1]
    pixel_count = inv_noise.shape[2]
    channel_width = inv_noise.shape[0]
    owner_index = lax.axis_index("blk")
    comp_index = lax.axis_index("comp")
    local_ids = lax.dynamic_slice_in_dim(cycle_slot, owner_index * cycle_count, cycle_count)
    local_lengths = cycle_len[local_ids]
    legendre_slot = legendre[:, :, cycle_slot]
    weights = mask_flags.astype(jnp.float32)
    own_beam = lax.dynamic_slice_in_dim(beam, comp_index * channel_width, channel_width, 0)
    stored = jax.vmap(cycle_table, in_axes=(None, 0, None))(m_values, local_lengths, pixel_count)
    solution = jnp.zeros_like(rhs)
    residual = rhs
    direction = rhs
    for iteration in range(ITERS):
        local_mix = jnp.einsum("fc,ckml->fkml", mixing, direction, precision=HIGHEST_PRECISION)
        summed = lax.psum(local_mix.astype(jnp.bfloat16), "comp").astype(jnp.float32)
        own_part = lax.dynamic_slice_in_dim(summed, comp_index * channel_width, channel_width, 0)
        blended = (own_part * own_beam[:, None, None, :]).astype(jnp.bfloat16)
        coeffs = jnp.einsum(
            "fkml,mlr->fkmr", blended, legendre_slot, preferred_element_type=jnp.float32
        ).astype(jnp.bfloat16)
        arrived = lax.all_to_all(coeffs, "blk", split_axis=3, concat_axis=2, tiled=True)
        sky_map = jnp.einsum("fkmq,qkmp->fqp", arrived, stored, preferred_element_type=jnp.float32)
        weighted = (weights[:, :, None] * inv_noise * sky_map).astype(jnp.bfloat16)
        projected = jnp.einsum(
            "fqp,qkmp->fkmq", weighted, stored, preferred_element_type=jnp.float32
        ).astype(jnp.bfloat16)
        returned = lax.all_to_all(projected, "blk", split_axis=2, concat_axis=3, tiled=True)
        harmonic = jnp.einsum(
            "fkms,mls->fkml", returned, legendre_slot, preferred_element_type=jnp.float32
        )
        everyone = lax.all_gather(
            harmonic.astype(jnp.bfloat16), ("comp", "lat"), axis=0, tiled=True
        ).astype(harmonic.dtype)
        stacked = everyone.reshape(
            (lax.axis_size("comp"), lax.axis_size("lat"), channel_width) + harmonic.shape[1:]
        )
        summed_bands = jnp.sum(stacked, axis=1).reshape((-1,) + harmonic.shape[1:])
        backward = jnp.einsum(
            "fc,fkml->ckml",
            mixing,
            summed_bands * beam[:, None, None, :],
            precision=HIGHEST_PRECISION,
        )
        applied = prior[:, None, None, :] * direction + backward
        totals = lax.psum(
            (
                jnp.sum(direction * applied),
                jnp.sum(residual * applied),
                jnp.sum(applied * applied),
                jnp.sum(residual * residual),
            ),
            ("blk", "comp"),
        )
        curvature, cross_term, square, norm_now = totals
        step_size = norm_now / curvature
        solution = solution + step_size * direction
        residual = residual - step_size * applied
        norm_next = norm_now - 2.0 * step_size * cross_term + step_size * step_size * square
        direction = residual + norm_next / norm_now * direction
    return (solution, residual)


def solution(mesh):
    in_specs = (
        P(("groups", "comp"), None, "blk", None),
        P("blk", None, "lat"),
        P(),
        P(None, "comp"),
        P("comp", None),
        P("comp", ("blk", "lat"), None),
        P("comp", ("blk", "lat")),
        P("lat"),
        P("lat"),
        P(),
    )
    out_specs = (P(("groups", "comp"), None, "blk", None), P(("groups", "comp"), None, "blk", None))
    return jax.shard_map(local, mesh=mesh, in_specs=in_specs, out_specs=out_specs, check_vma=False)
```

profile of v0, /device:TPU:0, one launch (start us, length us, event | category | flops | bytes accessed | tf_op | source)
XLA Modules:
  0.0 247.4 jit_solution(14166799779424596444)
XLA Ops:
  7.2 2.3 fusion.12
  13.4 22.6 %all-reduce.7.cloned.1.call-done = bf16[24,2,1,2048]{3,0,1,2:T(8,128)(2,1)} async-done(((bf16[24,2,1,2048]{3,0,1,2:T(8,128)(2,1)}), bf16[24,2,1,2048]{3,0,1,2:T(8,128)(2,1)}) %all-reduce.7.cloned.1.call-update) | async-done | bytes 196624 | tf_op jit(solution)/shard_map/psum | solution.py:43
  36.0 1.2 fusion.18
  37.8 4.6 %all-to-all-start = ((bf16[12,2,1,16]{0,1,2,3:T(2,128)(2,1)}), bf16[12,2,1,16]{0,1,2,3:T(2,128)(2,1)S(1)}, u32[]{:S(2)}, u32[]{:S(2)}) async-start(bf16[12,2,1,16]{0,1,2,3:T(2,128)(2,1)} %copy.87), calls=%async_computation | async-start | bytes 16384 | tf_op jit(solution)/shard_map/all_to_all | solution.py:49
  42.4 7.2 %select_convert_fusion.1 = (bf16[1,4,4,4096]{3,2,0,1:T(4,128)(2,1)S(1)}, bf16[1,4,4,4096]{3,2,0,1:T(4,128)(2,1)S(1)}) fusion(f32[4]{0:T(128)S(1)} %get-tuple-element.32, pred[4]{0:T(512)(128)(4,1)S(1)} %broadcast_compare_fusion, s32[4]{0:T(128)S(1)} %get-tuple-element.31, s32[4,4096]{1,0:T(4,128)S(1)} %broadcast_multiply_fusion, ...), kind=kLoop, calls=%fused_computation.88 | loop fusion | flops 983040 | bytes 344100 | tf_op jit(solution)/shard_map/convert.3
  51.3 5.1 %all-to-all-start.1 = ((bf16[12,2,4,4]{0,1,3,2:T(2,128)(2,1)}), bf16[12,2,4,4]{0,1,3,2:T(2,128)(2,1)S(1)}, u32[]{:S(2)}, u32[]{:S(2)}) async-start(bf16[12,2,4,4]{0,1,3,2:T(2,128)(2,1)} %copy.90), calls=%async_computation.1 | async-start | bytes 16384 | tf_op jit(solution)/shard_map/all_to_all | solution.py:55
  56.4 1.4 multiply_reduce_fusion.8
  57.8 4.2 %all-to-all-done.1 = bf16[12,2,4,4]{0,1,3,2:T(2,128)(2,1)S(1)} async-done(((bf16[12,2,4,4]{0,1,3,2:T(2,128)(2,1)}), bf16[12,2,4,4]{0,1,3,2:T(2,128)(2,1)S(1)}, u32[]{:S(2)}, u32[]{:S(2)}) %all-to-all-start.1) | async-done | bytes 800 | tf_op jit(solution)/shard_map/all_to_all | solution.py:55
  62.3 6.1 %all_gather.9 = bf16[48,2,1,2048]{3,1,2,0:T(2,128)(2,1)S(1)} all-gather(bf16[12,2,1,2048]{3,1,2,0:T(2,128)(2,1)S(1)} %copy.93), channel_id=1, replica_groups=mesh['groups'=2,'blk'=4,'comp'=2,'lat'=2] {'comp','lat'}, dimensions={0}, use_global_device_ids=true | all-gather | bytes 491520 | tf_op jit(solution)/shard_map/all_gather | solution.py:59
  69.9 1.5 multiply_reduce_fusion.5
  71.4 18.6 %all-reduce.2 = (f32[]{:T(128)}, f32[]{:T(128)}, f32[]{:T(128)}) all-reduce(f32[]{:T(128)} %multiply_reduce_fusion.8, f32[]{:T(128)} %get-tuple-element.15, f32[]{:T(128)} %get-tuple-element.14), channel_id=1, replica_groups=mesh['groups'=2,'blk'=4,'comp'=2,'lat'=2] {'blk','comp'}, use_global_device_ids=true, to_apply=%region_1.2 | all-reduce | flops 3 | bytes 24 | tf_op jit(solution)/shard_map/psum | solution.py:73
  95.3 20.3 %all-reduce.9.cloned.1.call-done = bf16[24,2,1,2048]{3,0,1,2:T(8,128)(2,1)} async-done(((bf16[24,2,1,2048]{3,0,1,2:T(8,128)(2,1)}), bf16[24,2,1,2048]{3,0,1,2:T(8,128)(2,1)}) %all-reduce.9.cloned.1.call-update) | async-done | bytes 196624 | tf_op jit(solution)/shard_map/psum | solution.py:43
  115.6 1.2 fusion.20
  116.8 10.0 %all_to_all.63 = bf16[12,2,1,16]{0,1,2,3:T(2,128)(2,1)S(1)} all-to-all(bf16[12,2,1,16]{0,1,2,3:T(2,128)(2,1)S(1)} %copy.100), channel_id=1, replica_groups=mesh['groups'=2,'blk'=4,'comp'=2,'lat'=2] {'blk'}, dimensions={3} | all-to-all | bytes 1536 | tf_op jit(solution)/shard_map/all_to_all | solution.py:49
  127.9 7.9 %all_to_all.64 = bf16[12,2,4,4]{0,1,3,2:T(2,128)(2,1)S(1)} all-to-all(bf16[12,2,4,4]{0,1,3,2:T(2,128)(2,1)S(1)} %copy.103), channel_id=1, replica_groups=mesh['groups'=2,'blk'=4,'comp'=2,'lat'=2] {'blk'}, dimensions={2} | all-to-all | bytes 1536 | tf_op jit(solution)/shard_map/all_to_all | solution.py:55
  136.2 6.3 %all_gather.10 = bf16[48,2,1,2048]{3,1,2,0:T(2,128)(2,1)S(1)} all-gather(bf16[12,2,1,2048]{3,1,2,0:T(2,128)(2,1)S(1)} %copy.106), channel_id=1, replica_groups=mesh['groups'=2,'blk'=4,'comp'=2,'lat'=2] {'comp','lat'}, dimensions={0}, use_global_device_ids=true | all-gather | bytes 491520 | tf_op jit(solution)/shard_map/all_gather | solution.py:59
  143.2 1.5 multiply_reduce_fusion.1
  144.6 18.7 %all-reduce.1 = (f32[]{:T(128)}, f32[]{:T(128)}, f32[]{:T(128)}, f32[]{:T(128)}) all-reduce(f32[]{:T(128)} %get-tuple-element.12, f32[]{:T(128)} %get-tuple-element.13, f32[]{:T(128)} %get-tuple-element.11, f32[]{:T(128)} %get-tuple-element.10), channel_id=1, replica_groups=mesh['groups'=2,'blk'=4,'comp'=2,'lat'=2] {'blk','comp'}, use_global_device_ids=true, to_apply=%region_7.8 | all-reduce | flops 4 | bytes 32 | tf_op jit(solution)/shard_map/psum | solution.py:73
  169.2 20.4 %all-reduce.11.cloned.1.call-done = bf16[24,2,1,2048]{3,0,1,2:T(8,128)(2,1)} async-done(((bf16[24,2,1,2048]{3,0,1,2:T(8,128)(2,1)}), bf16[24,2,1,2048]{3,0,1,2:T(8,128)(2,1)}) %all-reduce.11.cloned.1.call-update) | async-done | bytes 196624 | tf_op jit(solution)/shard_map/psum | solution.py:43
  190.8 10.0 %all_to_all.65 = bf16[12,2,1,16]{0,1,2,3:T(2,128)(2,1)S(1)} all-to-all(bf16[12,2,1,16]{0,1,2,3:T(2,128)(2,1)S(1)} %copy.109), channel_id=1, replica_groups=mesh['groups'=2,'blk'=4,'comp'=2,'lat'=2] {'blk'}, dimensions={3} | all-to-all | bytes 1536 | tf_op jit(solution)/shard_map/all_to_all | solution.py:49
  201.8 7.9 %all_to_all.66 = bf16[12,2,4,4]{0,1,3,2:T(2,128)(2,1)S(1)} all-to-all(bf16[12,2,4,4]{0,1,3,2:T(2,128)(2,1)S(1)} %copy.112), channel_id=1, replica_groups=mesh['groups'=2,'blk'=4,'comp'=2,'lat'=2] {'blk'}, dimensions={2} | all-to-all | bytes 1536 | tf_op jit(solution)/shard_map/all_to_all | solution.py:55
  210.1 6.1 %all_gather.11 = bf16[48,2,1,2048]{3,1,2,0:T(2,128)(2,1)S(1)} all-gather(bf16[12,2,1,2048]{3,1,2,0:T(2,128)(2,1)S(1)} %copy.115), channel_id=1, replica_groups=mesh['groups'=2,'blk'=4,'comp'=2,'lat'=2] {'comp','lat'}, dimensions={0}, use_global_device_ids=true | all-gather | bytes 491520 | tf_op jit(solution)/shard_map/all_gather | solution.py:59
  216.9 1.3 multiply_reduce_fusion
  218.3 18.6 %all-reduce = (f32[]{:T(128)}, f32[]{:T(128)}) all-reduce(f32[]{:T(128)} %get-tuple-element.25, f32[]{:T(128)} %get-tuple-element.35), channel_id=1, replica_groups=mesh['groups'=2,'blk'=4,'comp'=2,'lat'=2] {'blk','comp'}, use_global_device_ids=true, to_apply=%region_15.16 | all-reduce | flops 2 | bytes 16 | tf_op jit(solution)/shard_map/psum | solution.py:73
  (72 shorter events, 19.1 us)
Async XLA Ops:
  7.2 5.3 %copy-start = (bf16[1,2048,16]{1,2,0:T(8,128)(2,1)S(1)}, bf16[1,2048,16]{1,2,0:T(8,128)(2,1)}, u32[]{:S(2)}) copy-start(bf16[1,2048,16]{1,2,0:T(8,128)(2,1)} %param.11) | copy-start | bytes 196612
  7.2 28.8 %all-reduce.7.cloned.1.call-start = ((), (), s32[]{:S(2)}) async-start(), calls=%async_computation.6 | async-start | bytes 393216 | tf_op jit(solution)/shard_map/psum | solution.py:43
  9.6 0.7 copy-start.10
  10.3 0.7 copy-start.1
  11.7 0.7 copy-start.7
  12.4 0.9 copy-start.3
  13.4 36.3 %copy-start.8 = (f32[12,4,4096]{2,1,0:T(4,128)S(1)}, f32[12,4,4096]{2,1,0:T(4,128)}, u32[]{:S(2)}) copy-start(f32[12,4,4096]{2,1,0:T(4,128)} %param.15) | copy-start | bytes 2359300
  37.8 11.8 %all-to-all-start = ((bf16[12,2,1,16]{0,1,2,3:T(2,128)(2,1)}), bf16[12,2,1,16]{0,1,2,3:T(2,128)(2,1)S(1)}, u32[]{:S(2)}, u32[]{:S(2)}) async-start(bf16[12,2,1,16]{0,1,2,3:T(2,128)(2,1)} %copy.87), calls=%async_computation | async-start | bytes 16384 | tf_op jit(solution)/shard_map/all_to_all | solution.py:49
  42.4 7.2 %copy-start.6 = (s32[12,4]{0,1:T(4,128)S(1)}, s32[12,4]{0,1:T(4,128)}, u32[]{:S(2)}) copy-start(s32[12,4]{0,1:T(4,128)} %param.16) | copy-start | bytes 580
  49.7 6.8 %copy-start.2 = (f32[24,2,1,2048]{3,2,1,0:T(1,128)S(1)}, f32[24,2,1,2048]{3,2,1,0:T(1,128)}, u32[]{:S(2)}) copy-start(f32[24,2,1,2048]{3,2,1,0:T(1,128)} %param.10) | copy-start | bytes 1179652
  51.3 10.7 %all-to-all-start.1 = ((bf16[12,2,4,4]{0,1,3,2:T(2,128)(2,1)}), bf16[12,2,4,4]{0,1,3,2:T(2,128)(2,1)S(1)}, u32[]{:S(2)}, u32[]{:S(2)}) async-start(bf16[12,2,4,4]{0,1,3,2:T(2,128)(2,1)} %copy.90), calls=%async_computation.1 | async-start | bytes 16384 | tf_op jit(solution)/shard_map/all_to_all | solution.py:55
  56.4 59.2 %all-reduce.9.cloned.1.call-start = ((), (), s32[]{:S(2)}) async-start(), calls=%async_computation.7 | async-start | bytes 393216 | tf_op jit(solution)/shard_map/psum | solution.py:43
  68.9 0.9 copy-start.4
  69.0 0.9 copy-start.5
  95.2 94.3 %all-reduce.11.cloned.1.call-start = ((), (), s32[]{:S(2)}) async-start(), calls=%async_computation.8 | async-start | bytes 393216 | tf_op jit(solution)/shard_map/psum | solution.py:43
  168.0 32.8 %copy-start.9 = (f32[12,4,4096]{2,1,0:T(4,128)S(1)}, f32[12,4,4096]{2,1,0:T(4,128)}, u32[]{:S(2)}) copy-start(f32[12,4,4096]{2,1,0:T(4,128)} %param.15) | copy-start | bytes 2359300
Sparse Core Ops, SparseCore 0:
  10.8 25.1 all-reduce.6
  95.4 20.2 all-reduce.8
  169.3 20.2 all-reduce.10
where the time goes:
time: 248 us; the launch traced here: 247 us
  blocking collectives  110 us (44%)
  waiting for transfers between devices  67.6 us (27%)
  between operations  23.1 us (9%)
  matrix products  16.3 us (7%)
  other arithmetic  12.3 us (5%)
  starting transfers between devices  9.77 us (4%)
  local copies, waits for them, and re-layouts  8.04 us (3%)
    psum x3, waiting for transfers between devices, local(): lax.psum(local_mix.astype(jnp.bfloat16), 'comp').astype(jnp.float32)  63.3 us
    psum x3, blocking collectives, local(): lax.psum((jnp.sum(direction * applied), jnp.sum(residual * applied), jnp....  55.9 us
    all_to_all x2, blocking collectives, local(): lax.all_to_all(coeffs, 'blk', split_axis=3, concat_axis=2, tiled=True)  20 us
    all_gather x3, blocking collectives, local(): lax.all_gather(harmonic.astype(jnp.bfloat16), ('comp', 'lat'), axis=0, ti...  18.6 us
    all_to_all x2, blocking collectives, local(): lax.all_to_all(projected, 'blk', split_axis=2, concat_axis=3, tiled=True)  15.9 us
    another operation x1, other arithmetic  7.19 us
    unnamed x24, local copies, waits for them, and re-layouts  5.18 us
    all_to_all x1, starting transfers between devices, local(): lax.all_to_all(projected, 'blk', split_axis=2, concat_axis=3, tiled=True)  5.09 us
  transfers between devices with their start and end apart: 5, of which 4 were waited for; matrix products, arithmetic and copies ran while one was open for 4% of the time, Pallas kernels for 0%

commit v1 on v0

v1 whole, which is shorter than its diff:
```python
import functools
import math

import jax
import jax.numpy as jnp
from jax import lax
from jax.experimental import pallas as pl
from jax.experimental.pallas import tpu as pltpu
from jax.sharding import PartitionSpec as P

ITERS = 3
F32 = jnp.float32
BF16 = jnp.bfloat16
MESH = pl.DeviceIdType.MESH


def each(count, body):
    if count <= 16:
        for i in range(count):
            body(i)
    else:
        lax.fori_loop(0, count, lambda i, carry: (body(i), carry)[1], 0)


def mm(a, b, ca, cb):
    return lax.dot_general(a, b, (((ca,), (cb,)), ((), ())), preferred_element_type=F32)


def half_turn_trig(turns_num, length, inside):
    j = jnp.floor(2.0 * turns_num / length + 0.5)
    u = (2.0 * turns_num - j * length) / length * (math.pi / 2)
    u2 = u * u
    s = u + u * u2 * (-1.0 / 6 + u2 * (1.0 / 120 + u2 * (-1.0 / 5040 + u2 * (1.0 / 362880))))
    c = 1.0 + u2 * (-0.5 + u2 * (1.0 / 24 + u2 * (-1.0 / 720 + u2 * (1.0 / 40320))))
    odd = (j == 1.0) | (j == 3.0)
    cos_neg = (j == 1.0) | (j == 2.0)
    sin_neg = (j == 2.0) | (j == 3.0)
    cosine = jnp.where(odd, s, c)
    sine = jnp.where(odd, c, s)
    cosine = jnp.where(cos_neg, -cosine, cosine)
    sine = jnp.where(sin_neg, sine, -sine)
    return jnp.where(inside, cosine, 0.0), jnp.where(inside, sine, 0.0)


def kernel(
    dims,
    rhs_ref, leg_ref, beam_ref, mix_ref, mixt_ref, prior_ref, noise_ref, len_ref, slot_ref, m_ref,
    sol_ref, res_ref,
    leg_all, trig, gsend, gbuf, gplane, gt, xsend, xbuf, ssend, sbuf, xd, xr, d_ref, w_ref,
    leg_sems, g_sems, x_sems, s_sems,
):
    nb, nc, nl, fl, fp, qr, rb, mt, lmax, pmax, chunk = dims
    b, c, l = lax.axis_index("blk"), lax.axis_index("comp"), lax.axis_index("lat")
    n_all = nb * nc * nl
    n_x = nb * nc
    me = (b * nc + c) * nl + l
    me_x = b * nc + c
    two_fp = 2 * fp

    def peer_all(k):
        p = lax.rem(me + k, n_all)
        return p // (nc * nl), lax.rem(p // nl, nc), lax.rem(p, nl)

    def peer_x(k):
        p = lax.rem(me_x + k, n_x)
        return p // nc, lax.rem(p, nc)

    barrier = pltpu.get_barrier_semaphore()

    def greet(k):
        pb, pc, pq = peer_all(k + 1)
        pl.semaphore_signal(
            barrier, inc=1, device_id={"blk": pb, "comp": pc, "lat": pq}, device_id_type=MESH
        )

    each(n_all - 1, greet)

    def wait_bytes(ref, sem):
        pltpu.make_async_copy(ref, ref, sem).wait()

    rows = lax.broadcasted_iota(jnp.int32, (rb, rb), 1)
    hot = slot_ref[...] == rows
    own_leg = mm(hot.astype(F32).astype(BF16), leg_ref[...], 1, 1).astype(BF16)
    leg_all[l] = own_leg
    slot_len = jnp.sum(jnp.where(hot, len_ref[...], 0), axis=1, keepdims=True)
    row_ids = lax.broadcasted_iota(jnp.int32, (rb, 1), 0)

    pix = lax.broadcasted_iota(jnp.int32, (mt, pmax), 1)
    whole = m_ref[...] * (2 * pix + 1)
    whole_f = whole.astype(F32)
    for q in range(qr):
        n_i = jnp.sum(jnp.where(row_ids == b * qr + q, slot_len, 0), axis=0, keepdims=True)
        n_f = n_i.astype(F32)
        turns = jnp.floor(whole_f / (2.0 * n_f)).astype(jnp.int32)
        left = whole - turns * (2 * n_i)
        left = jnp.where(left < 0, left + 2 * n_i, left)
        left = jnp.where(left >= 2 * n_i, left - 2 * n_i, left)
        cosine, sine = half_turn_trig(left.astype(F32), n_f, pix < n_i)
        trig[q, 0] = cosine.astype(BF16).astype(F32)
        trig[q, 1] = sine.astype(BF16).astype(F32)

    def gram(m):
        pieces = []
        for q in range(qr):
            co, si = trig[q, 0], trig[q, 1]
            row_c = trig[q, 0, pl.ds(m, 1), :]
            row_s = trig[q, 1, pl.ds(m, 1), :]
            prod = jnp.concatenate([co * row_c, si * row_c, si * row_s, co * row_s], axis=0)
            out = mm(prod.astype(BF16), noise_ref[q], 1, 1)
            pieces += [out[: 2 * mt], out[2 * mt :]]
        width = 2 * qr * fp
        if width < 128:
            pieces.append(jnp.zeros((2 * mt, 128 - width), F32))
        gsend[m] = jnp.concatenate(pieces, axis=1)

    each(mt, gram)

    pl.semaphore_wait(barrier, n_all - 1)

    for k in range(1, nl):
        pltpu.make_async_remote_copy(
            leg_all.at[l], leg_all.at[l], leg_sems.at[0], leg_sems.at[1],
            device_id={"lat": lax.rem(l + k, nl)}, device_id_type=MESH,
        ).start()

    def send_g(k):
        pb, pc, pq = peer_all(k + 1)
        pltpu.make_async_remote_copy(
            gsend.at[pb], gbuf.at[me], g_sems.at[0], g_sems.at[1],
            device_id={"blk": pb, "comp": pc, "lat": pq}, device_id_type=MESH,
        ).start()

    each(n_all - 1, send_g)
    gbuf[me] = gsend[b]

    wait_bytes(leg_all.at[pl.ds(0, nl - 1)], leg_sems.at[1])

    def share_x(r):
        def send(k):
            pb, pc = peer_x(k + 1)
            pltpu.make_async_remote_copy(
                xsend.at[r], xbuf.at[r, me_x], x_sems.at[r, 0], x_sems.at[r, 1],
                device_id={"blk": pb, "comp": pc}, device_id_type=MESH,
            ).start()

        each(n_x - 1, send)
        xbuf[r, me_x] = xsend[r]

    leg_rows = nl * rb
    tile_rows = lax.broadcasted_iota(jnp.int32, (rb, 128), 0)
    tile_lanes = lax.broadcasted_iota(jnp.int32, (rb, 128), 1)
    pad_lane = lax.rem(tile_lanes, fp) >= fl
    first_k = lax.rem(tile_lanes, two_fp) < fp

    def mark(row):
        return (tile_rows == row) & (tile_lanes == fp - 1)

    def forward(values, where, legs, acc):
        bm = beam_ref[:, where]
        parts = [mm(mix_ref[...], v.astype(BF16), 1, 0) * bm for v in values]
        stack = jnp.concatenate(
            [parts[k][i * fp : (i + 1) * fp] for i in range(nc) for k in range(2)], axis=0
        ).astype(BF16)
        return acc + mm(legs, stack, 1, 1)

    def tile_of(acc):
        return jnp.concatenate([acc[i * rb : (i + 1) * rb] for i in range(nl)], axis=1)

    legs_of = lambda where: leg_all[:, :, where].reshape(leg_rows, chunk)

    acc = jnp.zeros((leg_rows, nc * two_fp), F32)
    for ch in range(lmax // chunk):
        where = pl.ds(ch * chunk, chunk)
        values = [rhs_ref[:, pl.ds(k * lmax + ch * chunk, chunk)] for k in range(2)]
        acc = forward(values, where, legs_of(where), acc)
    xsend[0] = tile_of(acc)
    share_x(0)

    wait_bytes(gbuf.at[pl.ds(0, n_all - 1)], g_sems.at[1])

    def place(i):
        for q in range(qr):
            gt[i * qr + q] = jnp.concatenate(
                [
                    gbuf[(i * nc + ic) * nl + il][:, q * two_fp : (q + 1) * two_fp]
                    for il in range(nl)
                    for ic in range(nc)
                ],
                axis=1,
            )

    each(nb, place)
    for p in range(2 * mt):
        gplane[p] = gt[:, p, :]

    def arrive_x(r):
        wait_bytes(xbuf.at[r, pl.ds(0, n_x - 1)], x_sems.at[r, 1])

    def weigh(r, step, ratio):
        def body(m, y):
            x = xbuf[r, m * nc]
            for i in range(1, nc):
                x = x + xbuf[r, m * nc + i]
            x = jnp.where(pad_lane, 0.0, x)
            if r == 0:
                xr[m] = x
                now = x
            else:
                rest = xr[m] - step * x
                now = rest + ratio * xd[m]
                xr[m] = rest
            xd[m] = now
            swapped = jnp.where(
                first_k, pltpu.roll(now, 128 - fp, 1), pltpu.roll(now, fp, 1)
            )
            return y + gplane[m] * now + gplane[mt + m] * swapped

        y = jnp.zeros((rb, 128), F32)
        if mt <= 16:
            for m in range(mt):
                y = body(m, y)
        else:
            y = lax.fori_loop(0, mt, body, y)
        width = nc * two_fp
        return jnp.concatenate(
            [y[:, i * width : (i + 1) * width] for i in range(nl)], axis=0
        ).astype(BF16)

    def total(value):
        return jnp.sum(jnp.sum(value, axis=0, keepdims=True), axis=1, keepdims=True)

    def scalars(tile):
        return [total(jnp.where(mark(i), tile, 0.0)) for i in range(4)]

    def coefficients_of_step(sums):
        curvature, cross, square, norm = sums
        step = norm / curvature
        nxt = norm - 2.0 * step * cross + step * step * square
        return step, nxt / norm

    step = ratio = None
    for it in range(ITERS):
        arrive_x(it)
        if it > 0:
            tile = xbuf[it, 0]
            for i in range(1, n_x):
                tile = tile + xbuf[it, i]
            step, ratio = coefficients_of_step(scalars(tile))
        y = weigh(it, step, ratio)
        last = it == ITERS - 1
        acc = jnp.zeros((leg_rows, nc * two_fp), F32)
        sums = [jnp.zeros((rhs_ref.shape[0], chunk), F32) for _ in range(4)]
        for ch in range(lmax // chunk):
            where = pl.ds(ch * chunk, chunk)
            legs = legs_of(where)
            spread = mm(y, legs, 0, 0)
            bm = beam_ref[:, where]
            values = []
            for k in range(2):
                both = pl.ds(k * lmax + ch * chunk, chunk)
                harm = jnp.concatenate(
                    [spread[i * two_fp + k * fp : i * two_fp + (k + 1) * fp] for i in range(nc)],
                    axis=0,
                )
                back = mm(mixt_ref[...], (harm * bm).astype(BF16), 1, 0)
                if it == 0:
                    d = rhs_ref[:, both]
                    rest = d
                else:
                    old = rhs_ref[:, both] if it == 1 else d_ref[:, both]
                    before = rhs_ref[:, both] if it == 1 else res_ref[:, both]
                    grown = step * old
                    sol_ref[:, both] = grown if it == 1 else sol_ref[:, both] + grown
                    rest = before - step * w_ref[:, both]
                    d = rest + ratio * old
                    res_ref[:, both] = rest
                    d_ref[:, both] = d
                w = prior_ref[:, where] * d + back
                w_ref[:, both] = w
                sums[0] = sums[0] + d * w
                sums[3] = sums[3] + rest * rest
                if not last:
                    sums[1] = sums[1] + rest * w
                    sums[2] = sums[2] + w * w
                values.append(w)
            if not last:
                acc = forward(values, where, legs, acc)
        if not last:
            tile = tile_of(acc)
            for i in range(4):
                tile = jnp.where(mark(i), total(sums[i]), tile)
            xsend[it + 1] = tile
            share_x(it + 1)

    small_rows = lax.broadcasted_iota(jnp.int32, (8, 128), 0)
    ssend[...] = jnp.where(
        small_rows == 0, total(sums[0]), jnp.where(small_rows == 1, total(sums[3]), 0.0)
    )

    def send_s(k):
        pb, pc = peer_x(k + 1)
        pltpu.make_async_remote_copy(
            ssend, sbuf.at[me_x], s_sems.at[0], s_sems.at[1],
            device_id={"blk": pb, "comp": pc}, device_id_type=MESH,
        ).start()

    each(n_x - 1, send_s)
    sbuf[me_x] = ssend[...]
    wait_bytes(sbuf.at[pl.ds(0, n_x - 1)], s_sems.at[1])
    sums = sbuf[0]
    for i in range(1, n_x):
        sums = sums + sbuf[i]
    step = sums[1:2, 0:1] / sums[0:1, 0:1]
    sol_ref[...] = sol_ref[...] + step * d_ref[...]
    res_ref[...] = res_ref[...] - step * w_ref[...]

    wait_bytes(leg_all.at[pl.ds(0, nl - 1)], leg_sems.at[0])
    wait_bytes(gbuf.at[pl.ds(0, n_all - 1)], g_sems.at[0])
    for r in range(ITERS):
        wait_bytes(xbuf.at[r, pl.ds(0, n_x - 1)], x_sems.at[r, 0])
    wait_bytes(sbuf.at[pl.ds(0, n_x - 1)], s_sems.at[0])


def local(
    rhs, legendre, beam, mixing, prior, inv_noise, mask_flags, cycle_len, cycle_slot, m_values
):
    nb, nc, nl = lax.axis_size("blk"), lax.axis_size("comp"), lax.axis_size("lat")
    fl, qr, pmax = inv_noise.shape
    lmax, rb = legendre.shape[1:]
    mt = m_values.shape[0]
    comps = rhs.shape[0]
    fp = 8 * (fl // 8 + 1)
    chunk = min(512, lmax)
    dims = (nb, nc, nl, fl, fp, qr, rb, mt, lmax, pmax, chunk)
    spare = ((0, 0), (0, fp - fl), (0, 0))
    beam_p = jnp.pad(beam.reshape(nc, fl, lmax), spare).reshape(nc * fp, lmax)
    mix_p = jnp.pad(mixing.reshape(nc, fl, comps), spare).reshape(nc * fp, comps).astype(BF16)
    noise = mask_flags.astype(F32)[:, :, None] * inv_noise
    noise = jnp.pad(jnp.transpose(noise, (1, 0, 2)), spare).astype(BF16)
    n_all, n_x = nb * nc * nl, nb * nc
    vm = pl.BlockSpec(memory_space=pltpu.VMEM)
    flat = jax.ShapeDtypeStruct((comps, 2 * lmax), F32)
    sol, res = pl.pallas_call(
        functools.partial(kernel, dims),
        out_shape=(flat, flat),
        in_specs=[vm] * 10,
        out_specs=(vm, vm),
        scratch_shapes=[
            pltpu.VMEM((nl, rb, lmax), BF16),
            pltpu.VMEM((qr, 2, mt, pmax), F32),
            pltpu.VMEM((mt, 2 * mt, 128), F32),
            pltpu.VMEM((n_all, 2 * mt, 128), F32),
            pltpu.VMEM((2 * mt, rb, 128), F32),
            pltpu.VMEM((rb, 2 * mt, 128), F32),
            pltpu.VMEM((ITERS, rb, 128), F32),
            pltpu.VMEM((ITERS, n_x, rb, 128), F32),
            pltpu.VMEM((8, 128), F32),
            pltpu.VMEM((n_x, 8, 128), F32),
            pltpu.VMEM((mt, rb, 128), F32),
            pltpu.VMEM((mt, rb, 128), F32),
            pltpu.VMEM((comps, 2 * lmax), F32),
            pltpu.VMEM((comps, 2 * lmax), F32),
            pltpu.SemaphoreType.DMA((2,)),
            pltpu.SemaphoreType.DMA((2,)),
            pltpu.SemaphoreType.DMA((ITERS, 2)),
            pltpu.SemaphoreType.DMA((2,)),
        ],
        compiler_params=pltpu.CompilerParams(collective_id=0, has_side_effects=True),
    )(
        rhs.reshape(comps, 2 * lmax),
        legendre[0],
        beam_p,
        mix_p,
        mix_p.T,
        prior,
        noise,
        cycle_len[None, :],
        cycle_slot[:, None],
        m_values[:, None],
    )
    return sol.reshape(rhs.shape), res.reshape(rhs.shape)


def solution(mesh):
    in_specs = (
        P(("groups", "comp"), None, "blk", None),
        P("blk", None, "lat"),
        P(),
        P(None, "comp"),
        P("comp", None),
        P("comp", ("blk", "lat"), None),
        P("comp", ("blk", "lat")),
        P("lat"),
        P("lat"),
        P(),
    )
    out_specs = (P(("groups", "comp"), None, "blk", None), P(("groups", "comp"), None, "blk", None))
    return jax.shard_map(local, mesh=mesh, in_specs=in_specs, out_specs=out_specs, check_vma=False)
```

time: 248 us -> 46.3 us (0.19)
  blocking collectives: 110 us -> 0 us
  waiting for transfers between devices: 67.6 us -> 0 us
  Pallas kernels: 0 us -> 31.7 us
  between operations: 23.1 us -> 0.69 us
  matrix products: 16.3 us -> 0 us
  other arithmetic: 12.3 us -> 2.32 us
  starting transfers between devices: 9.77 us -> 0 us
  local copies, waits for them, and re-layouts: 8.04 us -> 11.4 us
    psum x3 -> x0, waiting for transfers between devices: 63.3 us -> none  [local(): lax.psum(local_mix.astype(jnp.bfloat16), 'comp').astype(jnp.float32)]
    psum x3 -> x0, blocking collectives: 55.9 us -> none  [local(): lax.psum((jnp.sum(direction * applied), jnp.sum(residual * applied), jnp....]
    all_to_all x4 -> x0, blocking collectives: 35.8 us -> none  [the longest x2 20 us: local(): lax.all_to_all(coeffs, 'blk', split_axis=3, concat_axis=2, tiled=True)]
    pallas_call x0 -> x1, Pallas kernels: none -> 31.7 us  [local(): pl.pallas_call(functools.partial(kernel, dims), out_shape=(flat, flat), i...]
    all_gather x3 -> x0, blocking collectives: 18.6 us -> none  [local(): lax.all_gather(harmonic.astype(jnp.bfloat16), ('comp', 'lat'), axis=0, ti...]
    dot_general x15 -> x0, matrix products: 16.3 us -> none  [the longest x3 4.62 us: local(): jnp.einsum('fc,ckml->fkml', mixing, direction, precision=HIGHEST_PRECISION)]
    all_to_all x2 -> x0, starting transfers between devices: 9.69 us -> none  [the longest x1 5.09 us: local(): lax.all_to_all(projected, 'blk', split_axis=2, concat_axis=3, tiled=True)]
    another operation x1, other arithmetic: 7.19 us -> 0.01 us
  transfers between devices with their start and end apart: 5 -> 0, of which waited for: 4 -> 0; matrix products, arithmetic and copies ran while one was open for 4% -> 0% of each run, Pallas kernels for 0% -> 0%
where the time goes in v1:
time: 46.3 us; the launch traced here: 46 us
  Pallas kernels  31.7 us (68%)
  local copies, waits for them, and re-layouts  11.4 us (25%)
  other arithmetic  2.32 us (5%)
  between operations  0.69 us (1%)
    pallas_call x1, Pallas kernels, local(): pl.pallas_call(functools.partial(kernel, dims), out_shape=(flat, flat), i...  31.7 us
    reshape x2, local copies, waits for them, and re-layouts, local(): return (sol.reshape(rhs.shape), res.reshape(rhs.shape))  3.46 us
    unnamed x16, local copies, waits for them, and re-layouts  2.65 us
    broadcast_in_dim x1, local copies, waits for them, and re-layouts, local(): m_values[:, None]  1.31 us
    unnamed x1, other arithmetic  1.18 us
    reshape x1, local copies, waits for them, and re-layouts, local(): beam_p = jnp.pad(beam.reshape(nc, fl, lmax), spare).reshape(nc * fp, lmax)  1 us

profile of v1, /device:TPU:0, one launch (start us, length us, event | category | flops | bytes accessed | tf_op | source)
XLA Modules:
  0.0 46.0 jit_solution(13798724940917714935)
XLA Ops:
  0.6 0.0 copy-start.5
  0.6 0.7 %convert_element_type.14 = f32[12,4]{0,1:T(4,128)S(1)} convert(s32[12,4]{0,1:T(4,128)} %param.16) | non-fusion elementwise | flops 48 | bytes 384 | tf_op jit(solution)/shard_map/convert_element_type | solution.py:338
  1.3 1.3 %copy.24.m_ref = s32[4,1]{1,0:T(4,128)} copy(s32[4,1]{0,1:T(1,128)} %bitcast.19) | data formatting | bytes 32 | tf_op jit(solution)/shard_map/broadcast_in_dim | solution.py:379
  2.6 0.0 copy-done.5
  2.7 0.7 %copy.21 = bf16[32,24]{0,1:T(8,128)(2,1)} copy(bf16[32,24]{1,0:T(8,128)(2,1)S(1)} %bitcast.15) | data formatting | bytes 3072 | tf_op jit(solution)/shard_map/convert_element_type | solution.py:337
  3.4 0.0 copy-done.3
  3.4 0.7 %copy-done.6 = s32[16]{0:T(128)S(1)} copy-done((s32[16]{0:T(128)S(1)}, s32[16]{0:T(128)}, u32[]{:S(2)}) %copy-start.6) | copy-done | bytes 88
  4.0 0.7 %copy.23.slot_ref = s32[16,1]{1,0:T(8,128)} copy(s32[16,1]{0,1:T(1,128)S(1)} %bitcast.20) | data formatting | bytes 128 | tf_op jit(solution)/shard_map/broadcast_in_dim | solution.py:378
  4.7 1.0 %reshape.27 = f32[2,12,2048]{2,1,0:T(8,128)S(1)} reshape(f32[24,2048]{1,0:T(8,128)} %param.12) | data formatting | bytes 393216 | tf_op jit(solution)/shard_map/reshape | solution.py:336
  5.7 0.7 %pad.14 = f32[2,16,2048]{2,1,0:T(8,128)} pad(f32[2,12,2048]{2,1,0:T(8,128)S(1)} %reshape.27, f32[]{:T(128)} %constant.3.clone.1), padding=0_0x0_4x0_0 | pad | bytes 458756 | tf_op jit(solution)/shard_map/jit(_pad)/pad | solution.py:336
  6.4 0.0 copy-done.2
  6.4 1.2 %reduce = f32[24,2,2048]{2,1,0:T(2,128)S(1)} reduce(f32[24,2,1,2048]{3,2,1,0:T(1,128)S(1)} %copy-done.2, f32[]{:T(128)} %constant.15), dimensions={2}, to_apply=%param.10.reduce_sub_computation | reduce | bytes 786436 | tf_op args[0]
  7.6 1.0 %copy.27 = f32[3,8,2,2048]{3,1,2,0:T(8,128)} copy(f32[3,8,2,2048]{3,2,1,0:T(2,128)S(1)} %bitcast.13) | data formatting | bytes 786432
  8.6 0.0 copy-done
  8.6 0.4 fusion.1
  9.0 0.0 copy-start.4
  9.0 0.8 %pad.16.noise_ref = bf16[4,16,4096]{2,1,0:T(8,128)(2,1)} pad(bf16[4,12,4096]{2,1,0:T(8,128)(2,1)S(1)} %fusion.1, bf16[]{:T(256)} %constant.4.clone.1), padding=0_0x0_4x0_0 | pad | bytes 917506 | tf_op jit(solution)/shard_map/jit(_pad)/pad | solution.py:339
  9.9 0.0 copy-done.4
  9.9 1.0 %copy.20 = bf16[1,2048,16]{2,1,0:T(8,128)(2,1)} copy(bf16[1,2048,16]{1,2,0:T(8,128)(2,1)S(1)} %copy-done.4) | data formatting | bytes 131072 | tf_op args[1]
  10.9 31.7 %shard_map.113 = (f32[24,4096]{1,0:T(8,128)}, f32[24,4096]{1,0:T(8,128)}) custom-call(f32[24,4096]{1,0:T(8,128)} %bitcast.12, bf16[2048,16]{1,0:T(8,128)(2,1)} %bitcast.11, f32[32,2048]{1,0:T(8,128)} %bitcast.14, bf16[32,24]{1,0:T(8,128)(2,1)} %bitcast.16, bf16[24,32]{1,0:T(8,128)(2,1)} %bitcast.17, f32[24,2048]{1,0:T(8,128)} %prior_ref.1, ...), custom_call_target="tpu_custom_call" | custom-call | tf_op jit(solution)/shard_map/pallas_call | solution.py:343
  42.6 0.0 copy-start.1
  42.6 2.3 %reshape.32 = f32[24,2,1,2048]{3,2,1,0:T(1,128)} reshape(f32[24,4096]{1,0:T(8,128)} %get-tuple-element.4) | data formatting | bytes 786432 | tf_op jit(solution)/shard_map/reshape | solution.py:381
  44.8 0.0 copy-done.1
  44.8 1.2 %reshape.33 = f32[24,2,1,2048]{3,2,1,0:T(1,128)} reshape(f32[24,4096]{1,0:T(8,128)S(1)} %copy-done.1) | data formatting | bytes 786432 | tf_op jit(solution)/shard_map/reshape | solution.py:381
  (7 shorter events, 0.0 us)
Async XLA Ops:
  0.6 2.0 %copy-start.5 = (f32[24,24]{1,0:T(8,128)S(1)}, f32[24,24]{1,0:T(8,128)}, u32[]{:S(2)}) copy-start(f32[24,24]{1,0:T(8,128)} %param.13) | copy-start | bytes 6916
  2.7 0.7 %copy-start.3 = (bf16[2,16,24]{2,1,0:T(8,128)(2,1)}, bf16[2,16,24]{2,1,0:T(8,128)(2,1)S(1)}, u32[]{:S(2)}) copy-start(bf16[2,16,24]{2,1,0:T(8,128)(2,1)S(1)} %pad.15) | copy-start | bytes 4612
  3.4 0.7 %copy-start.6 = (s32[16]{0:T(128)S(1)}, s32[16]{0:T(128)}, u32[]{:S(2)}) copy-start(s32[16]{0:T(128)} %param.18) | copy-start | bytes 196
  4.7 1.7 %copy-start.2 = (f32[24,2,1,2048]{3,2,1,0:T(1,128)S(1)}, f32[24,2,1,2048]{3,2,1,0:T(1,128)}, u32[]{:S(2)}) copy-start(f32[24,2,1,2048]{3,2,1,0:T(1,128)} %param.10) | copy-start | bytes 1179652
  6.4 2.2 %copy-start = (f32[12,4,4096]{2,1,0:T(4,128)S(1)}, f32[12,4,4096]{2,1,0:T(4,128)}, u32[]{:S(2)}) copy-start(f32[12,4,4096]{2,1,0:T(4,128)} %param.15) | copy-start | bytes 2359300
  9.0 0.9 %copy-start.4 = (bf16[1,2048,16]{1,2,0:T(8,128)(2,1)S(1)}, bf16[1,2048,16]{1,2,0:T(8,128)(2,1)}, u32[]{:S(2)}) copy-start(bf16[1,2048,16]{1,2,0:T(8,128)(2,1)} %param.11) | copy-start | bytes 196612
  42.6 2.3 %copy-start.1 = (f32[24,4096]{1,0:T(8,128)S(1)}, f32[24,4096]{1,0:T(8,128)}, u32[]{:S(2)}) copy-start(f32[24,4096]{1,0:T(8,128)} %get-tuple-element.5) | copy-start | bytes 1179652

commit v2 on v1

--- a/solution.py
+++ b/solution.py
@@ -44,9 +44,10 @@
 
 def kernel(
     dims,
-    rhs_ref, leg_ref, beam_ref, mix_ref, mixt_ref, prior_ref, noise_ref, len_ref, slot_ref, m_ref,
-    sol_ref, res_ref,
-    leg_all, trig, gsend, gbuf, gplane, gt, xsend, xbuf, ssend, sbuf, xd, xr, d_ref, w_ref,
+    rhs_ref, leg_ref, beam_in, mix_in, prior_ref, noise_ref, mask_ref, len_ref, slot_ref,
+    slot_row, m_ref,
+    sol_out, res_out,
+    beam_ref, mix_pad, rhs_ref2, sol_ref, res_ref, leg_all, trig, noise_pad, gsend, gbuf, gplane, gt, xsend, xbuf, ssend, sbuf, xd, xr, d_ref, w_ref,
     leg_sems, g_sems, x_sems, s_sems,
 ):
     nb, nc, nl, fl, fp, qr, rb, mt, lmax, pmax, chunk = dims
@@ -78,19 +79,38 @@
     def wait_bytes(ref, sem):
         pltpu.make_async_copy(ref, ref, sem).wait()
 
-    rows = lax.broadcasted_iota(jnp.int32, (rb, rb), 1)
-    hot = slot_ref[...] == rows
-    own_leg = mm(hot.astype(F32).astype(BF16), leg_ref[...], 1, 1).astype(BF16)
-    leg_all[l] = own_leg
-    slot_len = jnp.sum(jnp.where(hot, len_ref[...], 0), axis=1, keepdims=True)
-    row_ids = lax.broadcasted_iota(jnp.int32, (rb, 1), 0)
+    hot = slot_row[...] == lax.broadcasted_iota(jnp.int32, (rb, rb), 0)
+    leg_all[l] = mm(hot.astype(F32).astype(BF16), leg_ref[...], 0, 0).astype(BF16)
+
+    beam_ref[...] = jnp.zeros_like(beam_ref)
+    mix_pad[...] = jnp.zeros_like(mix_pad)
+    for i in range(nc):
+        beam_ref[i * fp : i * fp + fl] = beam_in[i * fl : (i + 1) * fl]
+        mix_pad[i * fp : i * fp + fl] = mix_in[i * fl : (i + 1) * fl]
+    mix = mix_pad[...].astype(BF16)
+    rows_p = nc * fp
+    eye = lax.broadcasted_iota(jnp.int32, (rows_p, rows_p), 0) == lax.broadcasted_iota(
+        jnp.int32, (rows_p, rows_p), 1
+    )
+    mixt = mm(mix, eye.astype(F32).astype(BF16), 0, 0).astype(BF16)
+
+    def lane_block(k, at):
+        return (k * lmax + at) // 128
 
     pix = lax.broadcasted_iota(jnp.int32, (mt, pmax), 1)
-    whole = m_ref[...] * (2 * pix + 1)
+    m_rows = lax.broadcasted_iota(jnp.int32, (mt, 1), 0)
+    m_col = jnp.zeros((mt, 1), jnp.int32)
+    for m in range(mt):
+        m_col = jnp.where(m_rows == m, m_ref[m], m_col)
+    whole = m_col * (2 * pix + 1)
     whole_f = whole.astype(F32)
     for q in range(qr):
-        n_i = jnp.sum(jnp.where(row_ids == b * qr + q, slot_len, 0), axis=0, keepdims=True)
+        n_i = jnp.full((1, 1), len_ref[slot_ref[b * qr + q]], jnp.int32)
         n_f = n_i.astype(F32)
+        noise_q = jnp.concatenate(
+            [noise_ref[:, q, :], jnp.zeros((fp - fl, pmax), F32)], axis=0
+        )
+        noise_pad[q] = noise_q.astype(BF16)
         turns = jnp.floor(whole_f / (2.0 * n_f)).astype(jnp.int32)
         left = whole - turns * (2 * n_i)
         left = jnp.where(left < 0, left + 2 * n_i, left)
@@ -99,6 +119,13 @@
         trig[q, 0] = cosine.astype(BF16).astype(F32)
         trig[q, 1] = sine.astype(BF16).astype(F32)
 
+    masks = [
+        jnp.concatenate(
+            [mask_ref[q : q + 1, :].astype(F32), jnp.zeros((1, fp - fl), F32)], axis=1
+        )
+        for q in range(qr)
+    ]
+
     def gram(m):
         pieces = []
         for q in range(qr):
@@ -106,7 +133,7 @@
             row_c = trig[q, 0, pl.ds(m, 1), :]
             row_s = trig[q, 1, pl.ds(m, 1), :]
             prod = jnp.concatenate([co * row_c, si * row_c, si * row_s, co * row_s], axis=0)
-            out = mm(prod.astype(BF16), noise_ref[q], 1, 1)
+            out = mm(prod.astype(BF16), noise_pad[q], 1, 1) * masks[q]
             pieces += [out[: 2 * mt], out[2 * mt :]]
         width = 2 * qr * fp
         if width < 128:
@@ -157,7 +184,7 @@
 
     def forward(values, where, legs, acc):
         bm = beam_ref[:, where]
-        parts = [mm(mix_ref[...], v.astype(BF16), 1, 0) * bm for v in values]
+        parts = [mm(mix, v.astype(BF16), 1, 0) * bm for v in values]
         stack = jnp.concatenate(
             [parts[k][i * fp : (i + 1) * fp] for i in range(nc) for k in range(2)], axis=0
         ).astype(BF16)
@@ -171,7 +198,12 @@
     acc = jnp.zeros((leg_rows, nc * two_fp), F32)
     for ch in range(lmax // chunk):
         where = pl.ds(ch * chunk, chunk)
-        values = [rhs_ref[:, pl.ds(k * lmax + ch * chunk, chunk)] for k in range(2)]
+        values = []
+        for k in range(2):
+            at = lane_block(k, ch * chunk)
+            v = jnp.concatenate([rhs_ref[:, at + i, :] for i in range(chunk // 128)], axis=1)
+            rhs_ref2[:, pl.ds(k * lmax + ch * chunk, chunk)] = v
+            values.append(v)
         acc = forward(values, where, legs_of(where), acc)
     xsend[0] = tile_of(acc)
     share_x(0)
@@ -262,13 +294,13 @@
                     [spread[i * two_fp + k * fp : i * two_fp + (k + 1) * fp] for i in range(nc)],
                     axis=0,
                 )
-                back = mm(mixt_ref[...], (harm * bm).astype(BF16), 1, 0)
+                back = mm(mixt, (harm * bm).astype(BF16), 1, 0)
                 if it == 0:
-                    d = rhs_ref[:, both]
+                    d = rhs_ref2[:, both]
                     rest = d
                 else:
-                    old = rhs_ref[:, both] if it == 1 else d_ref[:, both]
-                    before = rhs_ref[:, both] if it == 1 else res_ref[:, both]
+                    old = rhs_ref2[:, both] if it == 1 else d_ref[:, both]
+                    before = rhs_ref2[:, both] if it == 1 else res_ref[:, both]
                     grown = step * old
                     sol_ref[:, both] = grown if it == 1 else sol_ref[:, both] + grown
                     rest = before - step * w_ref[:, both]
@@ -311,8 +343,10 @@
     for i in range(1, n_x):
         sums = sums + sbuf[i]
     step = sums[1:2, 0:1] / sums[0:1, 0:1]
-    sol_ref[...] = sol_ref[...] + step * d_ref[...]
-    res_ref[...] = res_ref[...] - step * w_ref[...]
+    for at in range(2 * lmax // 128):
+        lanes = pl.ds(at * 128, 128)
+        sol_out[:, at, :] = sol_ref[:, lanes] + step * d_ref[:, lanes]
+        res_out[:, at, :] = res_ref[:, lanes] - step * w_ref[:, lanes]
 
     wait_bytes(leg_all.at[pl.ds(0, nl - 1)], leg_sems.at[0])
     wait_bytes(gbuf.at[pl.ds(0, n_all - 1)], g_sems.at[0])
@@ -332,22 +366,24 @@
     fp = 8 * (fl // 8 + 1)
     chunk = min(512, lmax)
     dims = (nb, nc, nl, fl, fp, qr, rb, mt, lmax, pmax, chunk)
-    spare = ((0, 0), (0, fp - fl), (0, 0))
-    beam_p = jnp.pad(beam.reshape(nc, fl, lmax), spare).reshape(nc * fp, lmax)
-    mix_p = jnp.pad(mixing.reshape(nc, fl, comps), spare).reshape(nc * fp, comps).astype(BF16)
-    noise = mask_flags.astype(F32)[:, :, None] * inv_noise
-    noise = jnp.pad(jnp.transpose(noise, (1, 0, 2)), spare).astype(BF16)
     n_all, n_x = nb * nc * nl, nb * nc
     vm = pl.BlockSpec(memory_space=pltpu.VMEM)
-    flat = jax.ShapeDtypeStruct((comps, 2 * lmax), F32)
+    sm = pl.BlockSpec(memory_space=pltpu.SMEM)
+    flat = jax.ShapeDtypeStruct((comps, 2 * lmax // 128, 128), F32)
     sol, res = pl.pallas_call(
         functools.partial(kernel, dims),
         out_shape=(flat, flat),
-        in_specs=[vm] * 10,
+        in_specs=[vm] * 7 + [sm, sm, vm, sm],
         out_specs=(vm, vm),
         scratch_shapes=[
+            pltpu.VMEM((nc * fp, lmax), F32),
+            pltpu.VMEM((nc * fp, comps), F32),
+            pltpu.VMEM((comps, 2 * lmax), F32),
+            pltpu.VMEM((comps, 2 * lmax), F32),
+            pltpu.VMEM((comps, 2 * lmax), F32),
             pltpu.VMEM((nl, rb, lmax), BF16),
             pltpu.VMEM((qr, 2, mt, pmax), F32),
+            pltpu.VMEM((qr, fp, pmax), BF16),
             pltpu.VMEM((mt, 2 * mt, 128), F32),
             pltpu.VMEM((n_all, 2 * mt, 128), F32),
             pltpu.VMEM((2 * mt, rb, 128), F32),
@@ -367,16 +403,17 @@
         ],
         compiler_params=pltpu.CompilerParams(collective_id=0, has_side_effects=True),
     )(
-        rhs.reshape(comps, 2 * lmax),
-        legendre[0],
-        beam_p,
-        mix_p,
-        mix_p.T,
+        rhs.reshape(comps, 2 * lmax // 128, 128),
+        legendre[0].T,
+        beam,
+        mixing,
         prior,
-        noise,
-        cycle_len[None, :],
-        cycle_slot[:, None],
-        m_values[:, None],
+        inv_noise,
+        mask_flags.T,
+        cycle_len,
+        cycle_slot,
+        cycle_slot[None, :],
+        m_values,
     )
     return sol.reshape(rhs.shape), res.reshape(rhs.shape)
 

time: 46.3 us -> 35.8 us (0.77)
  local copies, waits for them, and re-layouts: 11.4 us -> 2.57 us
  other arithmetic: 2.32 us -> 0 us
  Pallas kernels: 31.7 us -> 32.4 us
    reshape x4 -> x0, local copies, waits for them, and re-layouts: 4.47 us -> none  [the longest x2 3.46 us: local(): return (sol.reshape(rhs.shape), res.reshape(rhs.shape))]
    broadcast_in_dim x2 -> x0, local copies, waits for them, and re-layouts: 1.98 us -> none  [the longest x1 1.31 us: local(): m_values[:, None]]
    pad x3 -> x0, local copies, waits for them, and re-layouts: 1.57 us -> none  [the longest x1 0.84 us: local(): noise = jnp.pad(jnp.transpose(noise, (1, 0, 2)), spare).astype(BF16)]
    unnamed x1 -> x0, other arithmetic: 1.18 us -> none
    pallas_call x1, Pallas kernels: 31.7 us -> 32.4 us  [local(): pl.pallas_call(functools.partial(kernel, dims), out_shape=(flat, flat), i...]
    convert_element_type x1 -> x0, other arithmetic: 0.69 us -> none  [local(): noise = mask_flags.astype(F32)[:, :, None] * inv_noise]
    convert_element_type x1 -> x0, local copies, waits for them, and re-layouts: 0.67 us -> none  [local(): jnp.pad(mixing.reshape(nc, fl, comps), spare).reshape(nc * fp, comps)]
    unnamed x16 -> x4, local copies, waits for them, and re-layouts: 2.65 us -> 2.57 us
where the time goes in v2:
time: 35.8 us; the launch traced here: 35.6 us
  Pallas kernels  32.4 us (91%)
  local copies, waits for them, and re-layouts  2.57 us (7%)
  between operations  0.65 us (2%)
    pallas_call x1, Pallas kernels, local(): pl.pallas_call(functools.partial(kernel, dims), out_shape=(flat, flat), i...  32.4 us
    unnamed x4, local copies, waits for them, and re-layouts  2.57 us

profile of v2, /device:TPU:0, one launch (start us, length us, event | category | flops | bytes accessed | tf_op | source)
XLA Modules:
  0.0 35.6 jit_solution(4246094325172716981)
XLA Ops:
  0.6 32.4 %shard_map.113 = (f32[24,32,128]{2,1,0:T(8,128)}, f32[24,32,128]{2,1,0:T(8,128)}) custom-call(f32[24,32,128]{2,1,0:T(8,128)} %bitcast.10, bf16[16,2048]{1,0:T(8,128)(2,1)} %bitcast.11, f32[24,2048]{1,0:T(8,128)} %beam_in.1, f32[24,24]{1,0:T(8,128)} %mix_in.1, f32[24,2048]{1,0:T(8,128)} %prior_ref.1, f32[12,4,4096]{2,1,0:T(4,128)} %noise_ref.1, ...), custom_call_target="tpu_custom_call" | custom-call | tf_op jit(solution)/shard_map/pallas_call | solution.py:373
  33.0 0.0 copy-start
  33.0 1.8 %copy.16 = f32[24,2,1,2048]{3,2,1,0:T(1,128)} copy(f32[24,2,1,2048]{3,2,1,0:T(1,128)} %bitcast.9) | data formatting | bytes 786432
  34.9 0.0 copy-done
  34.9 0.7 %copy.17 = f32[24,2,1,2048]{3,2,1,0:T(1,128)} copy(f32[24,2,1,2048]{3,2,1,0:T(1,128)S(1)} %bitcast.8) | data formatting | bytes 786432
Async XLA Ops:
  33.0 1.8 %copy-start = (f32[24,32,128]{2,1,0:T(8,128)S(1)}, f32[24,32,128]{2,1,0:T(8,128)}, u32[]{:S(2)}) copy-start(f32[24,32,128]{2,1,0:T(8,128)} %get-tuple-element.5) | copy-start | bytes 1179652

commit v3 on v2

--- a/solution.py
+++ b/solution.py
@@ -47,10 +47,10 @@
     rhs_ref, leg_ref, beam_in, mix_in, prior_ref, noise_ref, mask_ref, len_ref, slot_ref,
     slot_row, m_ref,
     sol_out, res_out,
-    beam_ref, mix_pad, rhs_ref2, sol_ref, res_ref, leg_all, trig, noise_pad, gsend, gbuf, gplane, gt, xsend, xbuf, ssend, sbuf, xd, xr, d_ref, w_ref,
-    leg_sems, g_sems, x_sems, s_sems,
+    beam_ref, mix_pad, rhs_ref2, sol_ref, res_ref, leg_all, trig, noise_pad, gsend, gbuf, gplane, gt, gall, gfull, gtf, gpf, hsend, hbuf, xsend, xbuf, ssend, sbuf, xd, xr, d_ref, w_ref,
+    leg_sems, g_sems, h_sems, f_sems, x_sems, s_sems,
 ):
-    nb, nc, nl, fl, fp, qr, rb, mt, lmax, pmax, chunk = dims
+    nb, nc, nl, fl, fp, qr, rb, mt, lmax, pmax, chunk, lean = dims
     b, c, l = lax.axis_index("blk"), lax.axis_index("comp"), lax.axis_index("lat")
     n_all = nb * nc * nl
     n_x = nb * nc
@@ -142,37 +142,6 @@
 
     each(mt, gram)
 
-    pl.semaphore_wait(barrier, n_all - 1)
-
-    for k in range(1, nl):
-        pltpu.make_async_remote_copy(
-            leg_all.at[l], leg_all.at[l], leg_sems.at[0], leg_sems.at[1],
-            device_id={"lat": lax.rem(l + k, nl)}, device_id_type=MESH,
-        ).start()
-
-    def send_g(k):
-        pb, pc, pq = peer_all(k + 1)
-        pltpu.make_async_remote_copy(
-            gsend.at[pb], gbuf.at[me], g_sems.at[0], g_sems.at[1],
-            device_id={"blk": pb, "comp": pc, "lat": pq}, device_id_type=MESH,
-        ).start()
-
-    each(n_all - 1, send_g)
-    gbuf[me] = gsend[b]
-
-    wait_bytes(leg_all.at[pl.ds(0, nl - 1)], leg_sems.at[1])
-
-    def share_x(r):
-        def send(k):
-            pb, pc = peer_x(k + 1)
-            pltpu.make_async_remote_copy(
-                xsend.at[r], xbuf.at[r, me_x], x_sems.at[r, 0], x_sems.at[r, 1],
-                device_id={"blk": pb, "comp": pc}, device_id_type=MESH,
-            ).start()
-
-        each(n_x - 1, send)
-        xbuf[r, me_x] = xsend[r]
-
     leg_rows = nl * rb
     tile_rows = lax.broadcasted_iota(jnp.int32, (rb, 128), 0)
     tile_lanes = lax.broadcasted_iota(jnp.int32, (rb, 128), 1)
@@ -195,7 +164,7 @@
 
     legs_of = lambda where: leg_all[:, :, where].reshape(leg_rows, chunk)
 
-    acc = jnp.zeros((leg_rows, nc * two_fp), F32)
+    acc = jnp.zeros((rb, nc * two_fp), F32)
     for ch in range(lmax // chunk):
         where = pl.ds(ch * chunk, chunk)
         values = []
@@ -204,9 +173,48 @@
             v = jnp.concatenate([rhs_ref[:, at + i, :] for i in range(chunk // 128)], axis=1)
             rhs_ref2[:, pl.ds(k * lmax + ch * chunk, chunk)] = v
             values.append(v)
-        acc = forward(values, where, legs_of(where), acc)
-    xsend[0] = tile_of(acc)
-    share_x(0)
+        acc = forward(values, where, leg_all[l, :, where], acc)
+    part = rb // nl
+    hsend[...] = jnp.concatenate([acc[i * part : (i + 1) * part] for i in range(nl)], axis=1)
+
+    pl.semaphore_wait(barrier, n_all - 1)
+
+    for k in range(1, nl):
+        pltpu.make_async_remote_copy(
+            leg_all.at[l], leg_all.at[l], leg_sems.at[0], leg_sems.at[1],
+            device_id={"lat": lax.rem(l + k, nl)}, device_id_type=MESH,
+        ).start()
+
+    def send_g(k):
+        pb, pc, pq = peer_all(k + 1)
+        pltpu.make_async_remote_copy(
+            gsend.at[pb], gbuf.at[me], g_sems.at[0], g_sems.at[1],
+            device_id={"blk": pb, "comp": pc, "lat": pq}, device_id_type=MESH,
+        ).start()
+        pltpu.make_async_remote_copy(
+            hsend, hbuf.at[me], h_sems.at[0], h_sems.at[1],
+            device_id={"blk": pb, "comp": pc, "lat": pq}, device_id_type=MESH,
+        ).start()
+
+    each(n_all - 1, send_g)
+    gbuf[me] = gsend[b]
+    hbuf[me] = hsend[...]
+
+    if lean:
+        for m in range(mt):
+            gall[m * 2 * mt : (m + 1) * 2 * mt] = gsend[m]
+        gfull[me_x] = gall[...].astype(BF16)
+
+    def share_x(r):
+        def send(k):
+            pb, pc = peer_x(k + 1)
+            pltpu.make_async_remote_copy(
+                xsend.at[r - 1], xbuf.at[r - 1, me_x], x_sems.at[r - 1, 0], x_sems.at[r - 1, 1],
+                device_id={"blk": pb, "comp": pc}, device_id_type=MESH,
+            ).start()
+
+        each(n_x - 1, send)
+        xbuf[r - 1, me_x] = xsend[r - 1]
 
     wait_bytes(gbuf.at[pl.ds(0, n_all - 1)], g_sems.at[1])
 
@@ -225,14 +233,72 @@
     for p in range(2 * mt):
         gplane[p] = gt[:, p, :]
 
+    def send_full():
+        def send(k):
+            pb, pc = peer_x(k + 1)
+            pltpu.make_async_remote_copy(
+                gfull.at[me_x], gfull.at[me_x], f_sems.at[0], f_sems.at[1],
+                device_id={"blk": pb, "comp": pc}, device_id_type=MESH,
+            ).start()
+
+        each(n_x - 1, send)
+
+    def place_full():
+        wait_bytes(gfull.at[pl.ds(0, n_x - 1)], f_sems.at[1])
+        for i in range(nb):
+            tiles = [gfull[i * nc + ic].astype(F32) for ic in range(nc)]
+            for q in range(qr):
+                pieces = [t[:, q * two_fp : (q + 1) * two_fp] for t in tiles]
+                pieces.append(jnp.zeros((2 * mt * mt, 128 - nc * two_fp), F32))
+                gtf[i * qr + q] = jnp.concatenate(pieces, axis=1)
+        for p in range(2 * mt * mt):
+            gpf[p] = gtf[:, p, :]
+
+    def own_band_form():
+        width = nc * two_fp
+        own = []
+        for m in range(mt):
+            x = xd[m]
+            for i in range(1, nl):
+                x = jnp.where(l == i, pltpu.roll(xd[m], 128 - i * width, 1), x)
+            own.append(x)
+        swapped = [
+            jnp.where(first_k, pltpu.roll(x, 128 - fp, 1), pltpu.roll(x, fp, 1)) for x in own
+        ]
+        form = jnp.zeros((rb, 128), F32)
+        for m in range(mt):
+            y = jnp.zeros((rb, 128), F32)
+            for o in range(mt):
+                y = y + gpf[m * 2 * mt + o] * own[o] + gpf[m * 2 * mt + mt + o] * swapped[o]
+            form = form + y * own[m]
+        return total(form)
+
     def arrive_x(r):
-        wait_bytes(xbuf.at[r, pl.ds(0, n_x - 1)], x_sems.at[r, 1])
+        if r == 0:
+            wait_bytes(hbuf.at[pl.ds(0, n_all - 1)], h_sems.at[1])
+        else:
+            wait_bytes(xbuf.at[r - 1, pl.ds(0, n_x - 1)], x_sems.at[r - 1, 1])
+
+    def first_tile(m):
+        bands = []
+        for il in range(nl):
+            t = hbuf[(m * nc) * nl + il]
+            for ic in range(1, nc):
+                t = t + hbuf[(m * nc + ic) * nl + il]
+            width = nc * two_fp
+            bands.append(
+                jnp.concatenate([t[:, i * width : (i + 1) * width] for i in range(nl)], axis=0)
+            )
+        return jnp.concatenate(bands, axis=1)
 
     def weigh(r, step, ratio):
         def body(m, y):
-            x = xbuf[r, m * nc]
-            for i in range(1, nc):
-                x = x + xbuf[r, m * nc + i]
+            if r == 0:
+                x = first_tile(m)
+            else:
+                x = xbuf[r - 1, m * nc]
+                for i in range(1, nc):
+                    x = x + xbuf[r - 1, m * nc + i]
             x = jnp.where(pad_lane, 0.0, x)
             if r == 0:
                 xr[m] = x
@@ -258,30 +324,54 @@
             [y[:, i * width : (i + 1) * width] for i in range(nl)], axis=0
         ).astype(BF16)
 
+    def fold(value):
+        out = value[:, :128]
+        for i in range(1, value.shape[1] // 128):
+            out = out + value[:, i * 128 : (i + 1) * 128]
+        return out
+
     def total(value):
         return jnp.sum(jnp.sum(value, axis=0, keepdims=True), axis=1, keepdims=True)
 
-    def scalars(tile):
-        return [total(jnp.where(mark(i), tile, 0.0)) for i in range(4)]
+    def scalars(tile, count):
+        return [total(jnp.where(mark(i), tile, 0.0)) for i in range(count)]
 
     def coefficients_of_step(sums):
-        curvature, cross, square, norm = sums
+        curvature, cross, square, norm = sums[:4]
         step = norm / curvature
         nxt = norm - 2.0 * step * cross + step * step * square
-        return step, nxt / norm
-
-    step = ratio = None
+        return step, nxt / norm, nxt
+
+    step = ratio = norm = smooth = None
     for it in range(ITERS):
         arrive_x(it)
         if it > 0:
-            tile = xbuf[it, 0]
+            tile = xbuf[it - 1, 0]
             for i in range(1, n_x):
-                tile = tile + xbuf[it, i]
-            step, ratio = coefficients_of_step(scalars(tile))
+                tile = tile + xbuf[it - 1, i]
+            sums = scalars(tile, 10 if it == ITERS - 1 and lean else 4)
+            step, ratio, norm = coefficients_of_step(sums)
         y = weigh(it, step, ratio)
         last = it == ITERS - 1
+        if last and lean:
+            rr, ww, dd, rw, rd, wd = sums[4:]
+            smooth = (
+                rr + step * step * ww + ratio * ratio * dd
+                - 2.0 * step * rw + 2.0 * ratio * rd - 2.0 * step * ratio * wd
+            )
+            form = own_band_form()
+            ssend[...] = jnp.broadcast_to(form, (8, 128))
+            for k in range(1, nl):
+                pltpu.make_async_remote_copy(
+                    ssend, sbuf.at[l], s_sems.at[0], s_sems.at[1],
+                    device_id={"lat": lax.rem(l + k, nl)}, device_id_type=MESH,
+                ).start()
+            sbuf[l] = ssend[...]
         acc = jnp.zeros((leg_rows, nc * two_fp), F32)
-        sums = [jnp.zeros((rhs_ref.shape[0], chunk), F32) for _ in range(4)]
+        weighted = lean and it == ITERS - 2
+        sums = [jnp.zeros((rhs_ref.shape[0], 128), F32) for _ in range(10 if weighted else 4)]
+        if it == 0:
+            wait_bytes(leg_all.at[pl.ds(0, nl - 1)], leg_sems.at[1])
         for ch in range(lmax // chunk):
             where = pl.ds(ch * chunk, chunk)
             legs = legs_of(where)
@@ -309,40 +399,58 @@
                     d_ref[:, both] = d
                 w = prior_ref[:, where] * d + back
                 w_ref[:, both] = w
-                sums[0] = sums[0] + d * w
-                sums[3] = sums[3] + rest * rest
+                if not (last and lean):
+                    sums[0] = sums[0] + fold(d * w)
+                    sums[3] = sums[3] + fold(rest * rest)
+                if weighted:
+                    pr, pw, pd = [prior_ref[:, where] * v for v in (rest, w, d)]
+                    for i, v in enumerate(
+                        (rest * pr, w * pw, d * pd, rest * pw, rest * pd, w * pd)
+                    ):
+                        sums[4 + i] = sums[4 + i] + fold(v)
                 if not last:
-                    sums[1] = sums[1] + rest * w
-                    sums[2] = sums[2] + w * w
+                    sums[1] = sums[1] + fold(rest * w)
+                    sums[2] = sums[2] + fold(w * w)
                 values.append(w)
             if not last:
                 acc = forward(values, where, legs, acc)
         if not last:
             tile = tile_of(acc)
-            for i in range(4):
+            for i in range(len(sums)):
                 tile = jnp.where(mark(i), total(sums[i]), tile)
-            xsend[it + 1] = tile
+            xsend[it] = tile
             share_x(it + 1)
-
-    small_rows = lax.broadcasted_iota(jnp.int32, (8, 128), 0)
-    ssend[...] = jnp.where(
-        small_rows == 0, total(sums[0]), jnp.where(small_rows == 1, total(sums[3]), 0.0)
-    )
-
-    def send_s(k):
-        pb, pc = peer_x(k + 1)
-        pltpu.make_async_remote_copy(
-            ssend, sbuf.at[me_x], s_sems.at[0], s_sems.at[1],
-            device_id={"blk": pb, "comp": pc}, device_id_type=MESH,
-        ).start()
-
-    each(n_x - 1, send_s)
-    sbuf[me_x] = ssend[...]
-    wait_bytes(sbuf.at[pl.ds(0, n_x - 1)], s_sems.at[1])
-    sums = sbuf[0]
-    for i in range(1, n_x):
-        sums = sums + sbuf[i]
-    step = sums[1:2, 0:1] / sums[0:1, 0:1]
+            if lean and it == 0:
+                send_full()
+            if lean and it == ITERS - 2:
+                place_full()
+
+    if lean:
+        wait_bytes(sbuf.at[pl.ds(0, nl - 1)], s_sems.at[1])
+        form = sbuf[0]
+        for i in range(1, nl):
+            form = form + sbuf[i]
+        step = norm / (smooth + form[0:1, 0:1])
+    else:
+        small_rows = lax.broadcasted_iota(jnp.int32, (8, 128), 0)
+        ssend[...] = jnp.where(
+            small_rows == 0, total(sums[0]), jnp.where(small_rows == 1, total(sums[3]), 0.0)
+        )
+
+        def send_s(k):
+            pb, pc = peer_x(k + 1)
+            pltpu.make_async_remote_copy(
+                ssend, sbuf.at[me_x], s_sems.at[0], s_sems.at[1],
+                device_id={"blk": pb, "comp": pc}, device_id_type=MESH,
+            ).start()
+
+        each(n_x - 1, send_s)
+        sbuf[me_x] = ssend[...]
+        wait_bytes(sbuf.at[pl.ds(0, n_x - 1)], s_sems.at[1])
+        sums = sbuf[0]
+        for i in range(1, n_x):
+            sums = sums + sbuf[i]
+        step = sums[1:2, 0:1] / sums[0:1, 0:1]
     for at in range(2 * lmax // 128):
         lanes = pl.ds(at * 128, 128)
         sol_out[:, at, :] = sol_ref[:, lanes] + step * d_ref[:, lanes]
@@ -350,9 +458,14 @@
 
     wait_bytes(leg_all.at[pl.ds(0, nl - 1)], leg_sems.at[0])
     wait_bytes(gbuf.at[pl.ds(0, n_all - 1)], g_sems.at[0])
-    for r in range(ITERS):
-        wait_bytes(xbuf.at[r, pl.ds(0, n_x - 1)], x_sems.at[r, 0])
-    wait_bytes(sbuf.at[pl.ds(0, n_x - 1)], s_sems.at[0])
+    wait_bytes(hbuf.at[pl.ds(0, n_all - 1)], h_sems.at[0])
+    for r in range(1, ITERS):
+        wait_bytes(xbuf.at[r - 1, pl.ds(0, n_x - 1)], x_sems.at[r - 1, 0])
+    if lean:
+        wait_bytes(gfull.at[pl.ds(0, n_x - 1)], f_sems.at[0])
+        wait_bytes(sbuf.at[pl.ds(0, nl - 1)], s_sems.at[0])
+    else:
+        wait_bytes(sbuf.at[pl.ds(0, n_x - 1)], s_sems.at[0])
 
 
 def local(
@@ -365,7 +478,9 @@
     comps = rhs.shape[0]
     fp = 8 * (fl // 8 + 1)
     chunk = min(512, lmax)
-    dims = (nb, nc, nl, fl, fp, qr, rb, mt, lmax, pmax, chunk)
+    lean = mt <= 8
+    full = 2 * mt * mt if lean else 16
+    dims = (nb, nc, nl, fl, fp, qr, rb, mt, lmax, pmax, chunk, lean)
     n_all, n_x = nb * nc * nl, nb * nc
     vm = pl.BlockSpec(memory_space=pltpu.VMEM)
     sm = pl.BlockSpec(memory_space=pltpu.SMEM)
@@ -388,8 +503,14 @@
             pltpu.VMEM((n_all, 2 * mt, 128), F32),
             pltpu.VMEM((2 * mt, rb, 128), F32),
             pltpu.VMEM((rb, 2 * mt, 128), F32),
-            pltpu.VMEM((ITERS, rb, 128), F32),
-            pltpu.VMEM((ITERS, n_x, rb, 128), F32),
+            pltpu.VMEM((full, 128), F32),
+            pltpu.VMEM((n_x, full, 128), BF16),
+            pltpu.VMEM((rb, full, 128), F32),
+            pltpu.VMEM((full, rb, 128), F32),
+            pltpu.VMEM((rb // nl, 128), F32),
+            pltpu.VMEM((n_all, rb // nl, 128), F32),
+            pltpu.VMEM((ITERS - 1, rb, 128), F32),
+            pltpu.VMEM((ITERS - 1, n_x, rb, 128), F32),
             pltpu.VMEM((8, 128), F32),
             pltpu.VMEM((n_x, 8, 128), F32),
             pltpu.VMEM((mt, rb, 128), F32),
@@ -398,7 +519,9 @@
             pltpu.VMEM((comps, 2 * lmax), F32),
             pltpu.SemaphoreType.DMA((2,)),
             pltpu.SemaphoreType.DMA((2,)),
-            pltpu.SemaphoreType.DMA((ITERS, 2)),
+            pltpu.SemaphoreType.DMA((2,)),
+            pltpu.SemaphoreType.DMA((2,)),
+            pltpu.SemaphoreType.DMA((ITERS - 1, 2)),
             pltpu.SemaphoreType.DMA((2,)),
         ],
         compiler_params=pltpu.CompilerParams(collective_id=0, has_side_effects=True),

time: 35.8 us -> 31.4 us (0.88)
  Pallas kernels: 32.4 us -> 28 us
    pallas_call x1, Pallas kernels: 32.4 us -> 28 us  [local(): pl.pallas_call(functools.partial(kernel, dims), out_shape=(flat, flat), i...]
where the time goes in v3:
time: 31.4 us; the launch traced here: 31.3 us
  Pallas kernels  28 us (89%)
  local copies, waits for them, and re-layouts  2.57 us (8%)
  between operations  0.65 us (2%)
    pallas_call x1, Pallas kernels, local(): pl.pallas_call(functools.partial(kernel, dims), out_shape=(flat, flat), i...  28 us
    unnamed x4, local copies, waits for them, and re-layouts  2.57 us

profile of v3, /device:TPU:0, one launch (start us, length us, event | category | flops | bytes accessed | tf_op | source)
XLA Modules:
  0.0 31.3 jit_solution(2550676503148154419)
XLA Ops:
  0.6 28.0 %shard_map.113 = (f32[24,32,128]{2,1,0:T(8,128)}, f32[24,32,128]{2,1,0:T(8,128)}) custom-call(f32[24,32,128]{2,1,0:T(8,128)} %bitcast.10, bf16[16,2048]{1,0:T(8,128)(2,1)} %bitcast.11, f32[24,2048]{1,0:T(8,128)} %beam_in.1, f32[24,24]{1,0:T(8,128)} %mix_in.1, f32[24,2048]{1,0:T(8,128)} %prior_ref.1, f32[12,4,4096]{2,1,0:T(4,128)} %noise_ref.1, ...), custom_call_target="tpu_custom_call" | custom-call | tf_op jit(solution)/shard_map/pallas_call | solution.py:488
  28.7 0.0 copy-start
  28.7 1.8 %copy.16 = f32[24,2,1,2048]{3,2,1,0:T(1,128)} copy(f32[24,2,1,2048]{3,2,1,0:T(1,128)} %bitcast.9) | data formatting | bytes 786432
  30.5 0.0 copy-done
  30.5 0.7 %copy.17 = f32[24,2,1,2048]{3,2,1,0:T(1,128)} copy(f32[24,2,1,2048]{3,2,1,0:T(1,128)S(1)} %bitcast.8) | data formatting | bytes 786432
Async XLA Ops:
  28.7 1.8 %copy-start = (f32[24,32,128]{2,1,0:T(8,128)S(1)}, f32[24,32,128]{2,1,0:T(8,128)}, u32[]{:S(2)}) copy-start(f32[24,32,128]{2,1,0:T(8,128)} %get-tuple-element.5) | copy-start | bytes 1179652

commit v4 on v3

--- a/solution.py
+++ b/solution.py
@@ -46,9 +46,9 @@
     dims,
     rhs_ref, leg_ref, beam_in, mix_in, prior_ref, noise_ref, mask_ref, len_ref, slot_ref,
     slot_row, m_ref,
-    sol_out, res_out,
-    beam_ref, mix_pad, rhs_ref2, sol_ref, res_ref, leg_all, trig, noise_pad, gsend, gbuf, gplane, gt, gall, gfull, gtf, gpf, hsend, hbuf, xsend, xbuf, ssend, sbuf, xd, xr, d_ref, w_ref,
-    leg_sems, g_sems, h_sems, f_sems, x_sems, s_sems,
+    sol_ref, dir_out, res_ref, w_ref, step_out,
+    beam_ref, mix_pad, rhs_ref2, leg_all, trig, noise_pad, gsend, gbuf, gplane, gt, gall, gfull, gtf, gpf, msend, xsend, xbuf, ssend, sbuf, xd, xr, keep,
+    leg_sems, g_sems, f_sems, x_sems, s_sems,
 ):
     nb, nc, nl, fl, fp, qr, rb, mt, lmax, pmax, chunk, lean = dims
     b, c, l = lax.axis_index("blk"), lax.axis_index("comp"), lax.axis_index("lat")
@@ -175,7 +175,12 @@
             values.append(v)
         acc = forward(values, where, leg_all[l, :, where], acc)
     part = rb // nl
-    hsend[...] = jnp.concatenate([acc[i * part : (i + 1) * part] for i in range(nl)], axis=1)
+    first = jnp.concatenate([acc[i * part : (i + 1) * part] for i in range(nl)], axis=1)
+
+    def pack(m):
+        msend[m] = jnp.concatenate([gsend[m], first], axis=0).astype(BF16)
+
+    each(mt, pack)
 
     pl.semaphore_wait(barrier, n_all - 1)
 
@@ -188,17 +193,12 @@
     def send_g(k):
         pb, pc, pq = peer_all(k + 1)
         pltpu.make_async_remote_copy(
-            gsend.at[pb], gbuf.at[me], g_sems.at[0], g_sems.at[1],
+            msend.at[pb], gbuf.at[me], g_sems.at[0], g_sems.at[1],
             device_id={"blk": pb, "comp": pc, "lat": pq}, device_id_type=MESH,
         ).start()
-        pltpu.make_async_remote_copy(
-            hsend, hbuf.at[me], h_sems.at[0], h_sems.at[1],
-            device_id={"blk": pb, "comp": pc, "lat": pq}, device_id_type=MESH,
-        ).start()
 
     each(n_all - 1, send_g)
-    gbuf[me] = gsend[b]
-    hbuf[me] = hsend[...]
+    gbuf[me] = msend[b]
 
     if lean:
         for m in range(mt):
@@ -222,7 +222,7 @@
         for q in range(qr):
             gt[i * qr + q] = jnp.concatenate(
                 [
-                    gbuf[(i * nc + ic) * nl + il][:, q * two_fp : (q + 1) * two_fp]
+                    gbuf[(i * nc + ic) * nl + il][: 2 * mt, q * two_fp : (q + 1) * two_fp].astype(F32)
                     for il in range(nl)
                     for ic in range(nc)
                 ],
@@ -274,17 +274,15 @@
         return total(form)
 
     def arrive_x(r):
-        if r == 0:
-            wait_bytes(hbuf.at[pl.ds(0, n_all - 1)], h_sems.at[1])
-        else:
+        if r > 0:
             wait_bytes(xbuf.at[r - 1, pl.ds(0, n_x - 1)], x_sems.at[r - 1, 1])
 
     def first_tile(m):
         bands = []
         for il in range(nl):
-            t = hbuf[(m * nc) * nl + il]
+            t = gbuf[(m * nc) * nl + il][2 * mt :].astype(F32)
             for ic in range(1, nc):
-                t = t + hbuf[(m * nc + ic) * nl + il]
+                t = t + gbuf[(m * nc + ic) * nl + il][2 * mt :].astype(F32)
             width = nc * two_fp
             bands.append(
                 jnp.concatenate([t[:, i * width : (i + 1) * width] for i in range(nl)], axis=0)
@@ -323,6 +321,13 @@
         return jnp.concatenate(
             [y[:, i * width : (i + 1) * width] for i in range(nl)], axis=0
         ).astype(BF16)
+
+    def put(slot, ref, last, both, at, value):
+        if not last:
+            keep[slot, :, both] = value
+            return
+        for i in range(chunk // 128):
+            ref[:, at + i, :] = value[:, i * 128 : (i + 1) * 128]
 
     def fold(value):
         out = value[:, :128]
@@ -380,6 +385,7 @@
             values = []
             for k in range(2):
                 both = pl.ds(k * lmax + ch * chunk, chunk)
+                first_lane = lane_block(k, ch * chunk)
                 harm = jnp.concatenate(
                     [spread[i * two_fp + k * fp : i * two_fp + (k + 1) * fp] for i in range(nc)],
                     axis=0,
@@ -389,16 +395,16 @@
                     d = rhs_ref2[:, both]
                     rest = d
                 else:
-                    old = rhs_ref2[:, both] if it == 1 else d_ref[:, both]
-                    before = rhs_ref2[:, both] if it == 1 else res_ref[:, both]
+                    old = rhs_ref2[:, both] if it == 1 else keep[2, :, both]
+                    before = rhs_ref2[:, both] if it == 1 else keep[1, :, both]
                     grown = step * old
-                    sol_ref[:, both] = grown if it == 1 else sol_ref[:, both] + grown
-                    rest = before - step * w_ref[:, both]
+                    put(0, sol_ref, last, both, first_lane, grown if it == 1 else keep[0, :, both] + grown)
+                    rest = before - step * keep[3, :, both]
                     d = rest + ratio * old
-                    res_ref[:, both] = rest
-                    d_ref[:, both] = d
+                    put(1, res_ref, last, both, first_lane, rest)
+                    put(2, dir_out, last, both, first_lane, d)
                 w = prior_ref[:, where] * d + back
-                w_ref[:, both] = w
+                put(3, w_ref, last, both, first_lane, w)
                 if not (last and lean):
                     sums[0] = sums[0] + fold(d * w)
                     sums[3] = sums[3] + fold(rest * rest)
@@ -451,14 +457,10 @@
         for i in range(1, n_x):
             sums = sums + sbuf[i]
         step = sums[1:2, 0:1] / sums[0:1, 0:1]
-    for at in range(2 * lmax // 128):
-        lanes = pl.ds(at * 128, 128)
-        sol_out[:, at, :] = sol_ref[:, lanes] + step * d_ref[:, lanes]
-        res_out[:, at, :] = res_ref[:, lanes] - step * w_ref[:, lanes]
+    step_out[...] = jnp.broadcast_to(step, (8, 128))
 
     wait_bytes(leg_all.at[pl.ds(0, nl - 1)], leg_sems.at[0])
     wait_bytes(gbuf.at[pl.ds(0, n_all - 1)], g_sems.at[0])
-    wait_bytes(hbuf.at[pl.ds(0, n_all - 1)], h_sems.at[0])
     for r in range(1, ITERS):
         wait_bytes(xbuf.at[r - 1, pl.ds(0, n_x - 1)], x_sems.at[r - 1, 0])
     if lean:
@@ -485,39 +487,34 @@
     vm = pl.BlockSpec(memory_space=pltpu.VMEM)
     sm = pl.BlockSpec(memory_space=pltpu.SMEM)
     flat = jax.ShapeDtypeStruct((comps, 2 * lmax // 128, 128), F32)
-    sol, res = pl.pallas_call(
+    sol, direction, res, applied, step = pl.pallas_call(
         functools.partial(kernel, dims),
-        out_shape=(flat, flat),
+        out_shape=(flat,) * 4 + (jax.ShapeDtypeStruct((8, 128), F32),),
         in_specs=[vm] * 7 + [sm, sm, vm, sm],
-        out_specs=(vm, vm),
+        out_specs=(vm,) * 5,
         scratch_shapes=[
             pltpu.VMEM((nc * fp, lmax), F32),
             pltpu.VMEM((nc * fp, comps), F32),
-            pltpu.VMEM((comps, 2 * lmax), F32),
-            pltpu.VMEM((comps, 2 * lmax), F32),
             pltpu.VMEM((comps, 2 * lmax), F32),
             pltpu.VMEM((nl, rb, lmax), BF16),
             pltpu.VMEM((qr, 2, mt, pmax), F32),
             pltpu.VMEM((qr, fp, pmax), BF16),
             pltpu.VMEM((mt, 2 * mt, 128), F32),
-            pltpu.VMEM((n_all, 2 * mt, 128), F32),
+            pltpu.VMEM((n_all, 2 * mt + rb // nl, 128), BF16),
             pltpu.VMEM((2 * mt, rb, 128), F32),
             pltpu.VMEM((rb, 2 * mt, 128), F32),
             pltpu.VMEM((full, 128), F32),
             pltpu.VMEM((n_x, full, 128), BF16),
             pltpu.VMEM((rb, full, 128), F32),
             pltpu.VMEM((full, rb, 128), F32),
-            pltpu.VMEM((rb // nl, 128), F32),
-            pltpu.VMEM((n_all, rb // nl, 128), F32),
+            pltpu.VMEM((mt, 2 * mt + rb // nl, 128), BF16),
             pltpu.VMEM((ITERS - 1, rb, 128), F32),
             pltpu.VMEM((ITERS - 1, n_x, rb, 128), F32),
             pltpu.VMEM((8, 128), F32),
             pltpu.VMEM((n_x, 8, 128), F32),
             pltpu.VMEM((mt, rb, 128), F32),
             pltpu.VMEM((mt, rb, 128), F32),
-            pltpu.VMEM((comps, 2 * lmax), F32),
-            pltpu.VMEM((comps, 2 * lmax), F32),
-            pltpu.SemaphoreType.DMA((2,)),
+            pltpu.VMEM((4, comps, 2 * lmax), F32),
             pltpu.SemaphoreType.DMA((2,)),
             pltpu.SemaphoreType.DMA((2,)),
             pltpu.SemaphoreType.DMA((2,)),
@@ -538,6 +535,9 @@
         cycle_slot[None, :],
         m_values,
     )
+    step = step[0, 0]
+    sol = sol + step * direction
+    res = res - step * applied
     return sol.reshape(rhs.shape), res.reshape(rhs.shape)
 
 

time: 31.4 us -> 33.5 us (1.067)
  other arithmetic: 0 us -> 3.02 us
  local copies, waits for them, and re-layouts: 2.57 us -> 1.25 us
  Pallas kernels: 28 us -> 28.4 us
    sub x0 -> x1, other arithmetic: none -> 3.02 us  [local(): res = res - step * applied]
    unnamed x4 -> x0, local copies, waits for them, and re-layouts: 2.57 us -> none
    slice x0 -> x1, local copies, waits for them, and re-layouts: none -> 1.25 us  [local(): step = step[0, 0]]
where the time goes in v4:
time: 33.5 us; the launch traced here: 33.3 us
  Pallas kernels  28.4 us (85%)
  other arithmetic  3.02 us (9%)
  local copies, waits for them, and re-layouts  1.25 us (4%)
  between operations  0.64 us (2%)
    pallas_call x1, Pallas kernels, local(): pl.pallas_call(functools.partial(kernel, dims), out_shape=(flat,) * 4 + (...  28.4 us
    sub x1, other arithmetic, local(): res = res - step * applied  3.02 us
    slice x1, local copies, waits for them, and re-layouts, local(): step = step[0, 0]  1.25 us

profile of v4, /device:TPU:0, one launch (start us, length us, event | category | flops | bytes accessed | tf_op | source)
XLA Modules:
  0.0 33.3 jit_solution(15691620949360733019)
XLA Ops:
  0.6 28.4 %shard_map.113 = (f32[24,32,128]{2,1,0:T(8,128)}, f32[24,32,128]{2,1,0:T(8,128)}, f32[24,32,128]{2,1,0:T(8,128)}, f32[24,32,128]{2,1,0:T(8,128)}, f32[8,128]{1,0:T(8,128)}) custom-call(f32[24,32,128]{2,1,0:T(8,128)} %bitcast.11, bf16[16,2048]{1,0:T(8,128)(2,1)} %bitcast.12, f32[24,2048]{1,0:T(8,128)} %beam_in.1, f32[24,24]{1,0:T(8,128)} %mix_in.1, ...), custom_call_target="tpu_custom_call" | custom-call | tf_op jit(solution)/shard_map/pallas_call | solution.py:490
  29.0 1.2 %slice.3 = f32[1,1]{1,0:T(1,128)} slice(f32[8,128]{1,0:T(8,128)} %get-tuple-element.8), slice={[0:1], [0:1]} | slice | bytes 8 | tf_op jit(solution)/shard_map/slice | solution.py:538
  30.3 3.0 %multiply_subtract_fusion = (f32[24,32,128]{2,1,0:T(8,128)}, f32[24,32,128]{2,1,0:T(8,128)}) fusion(f32[24,32,128]{2,1,0:T(8,128)} %get-tuple-element.10, f32[24,32,128]{2,1,0:T(8,128)} %get-tuple-element.11, f32[]{:T(128)} %bitcast.5, f32[24,32,128]{2,1,0:T(8,128)} %get-tuple-element.7, f32[24,32,128]{2,1,0:T(8,128)} %get-tuple-element.9), kind=kLoop, calls=%fused_computation | loop fusion | flops 393216 | bytes 2359300 | tf_op jit(solution)/shard_map/sub | solution.py:540
